TPU v7x, 256 devices: a whole 4x4x8 slice. The times are simulated.
256 devices in a mesh: gx: 8 (over y, core), gy: 32 (over x, z).
Axes of the slice: x: 4, y: 4, z: 8, core: 2. Of those that a mesh axis runs over, the one named last changes fastest.
Arguments:
- right_side: float32 [64, 512, 256], P('gx', 'gy'), may hold values from -8 to 8
- velocity: float32 [3, 64, 512, 256], P(None, 'gx', 'gy'), may hold values from 0.1 to 3
- deflation: bfloat16 [32, 64, 512, 256], P(None, 'gx', 'gy'), may hold values from -0.1875 to 0.1875
- inverse_rows: float32 [8192, 8192], P(('gx', 'gy')), may hold values from -0.0625 to 0.0625
Outputs:
- solution_field: float32 [64, 512, 256], P('gx', 'gy')
- residual: float32 [64, 512, 256], P('gx', 'gy')
All inputs are finite; a program needn't handle non-finite values.
Results may differ from a plain program's by a relative error of at most 0.005.
Values sent between devices are 32-bit elements; how exact they have to be, the bound alone decides.
A program may use at most 64 MiB of HBM per device.

v0:
```python
import jax
import jax.numpy as jnp
from jax import lax
from jax.sharding import PartitionSpec as P

KD = 32
DEPTH = 2
CHEB = 4
cheb_center = 1.0
cheb_radius = 0.9


def with_halo(block, sides, width):
    for axis, dim in sides:
        count = lax.axis_size(axis)
        forward = [(i, i + 1) for i in range(count - 1)]
        backward = [(target, source) for source, target in forward]
        low = lax.ppermute(
            lax.slice_in_dim(block, block.shape[dim] - width, None, axis=dim), axis, forward
        )
        high = lax.ppermute(lax.slice_in_dim(block, 0, width, axis=dim), axis, backward)
        block = jnp.concatenate([low, block, high], axis=dim)
    return block


def upwind(padded, velocity):
    centre = padded[1:-1, 1:-1, 1:-1]
    diagonal = 6.0 + velocity[0] + velocity[1] + velocity[2]
    beside = padded[2:, 1:-1, 1:-1] + (1.0 + velocity[0]) * padded[:-2, 1:-1, 1:-1]
    beside = beside + padded[1:-1, 2:, 1:-1] + (1.0 + velocity[1]) * padded[1:-1, :-2, 1:-1]
    beside = beside + padded[1:-1, 1:-1, 2:] + (1.0 + velocity[2]) * padded[1:-1, 1:-1, :-2]
    return diagonal * centre - beside


def box_apply(field, velocity):
    return upwind(jnp.pad(field, 1), velocity)


def chebyshev(source, velocity, inside):
    inverse_diag = 1.0 / (6.0 + velocity[0] + velocity[1] + velocity[2])
    sigma_ratio = cheb_center / cheb_radius
    rho_now = 1.0 / sigma_ratio
    update = inverse_diag * source / cheb_center * inside
    estimate = update
    remainder = source
    for sweep_index in range(CHEB - 1):
        remainder = remainder - box_apply(update, velocity)
        rho_next = 1.0 / (2.0 * sigma_ratio - rho_now)
        update = (
            rho_next * rho_now * update + 2.0 * rho_next / cheb_radius * inverse_diag * remainder
        ) * inside
        estimate = estimate + update
        rho_now = rho_next
    return estimate


def apply_global(field, velocity):
    padded = with_halo(field, (("gx", 0), ("gy", 1)), 1)
    padded = jnp.pad(padded, ((0, 0), (0, 0), (1, 1)))
    return upwind(padded, velocity)


def precondition(residual, velocity, wide_velocity, flat_vectors, inverse_rows, inside):
    size_x, size_y, size_z = residual.shape
    coarse = jnp.dot(
        flat_vectors, residual.astype(jnp.bfloat16).reshape(-1), preferred_element_type=jnp.float32
    )
    gathered = lax.all_gather(coarse, ("gx", "gy"), axis=0, tiled=True)
    solved = jnp.dot(inverse_rows, gathered, precision=lax.Precision.HIGHEST)
    solved = solved.astype(jnp.bfloat16)
    correction = jnp.dot(solved, flat_vectors, preferred_element_type=jnp.float32).reshape(
        size_x, size_y, size_z
    )
    remaining = residual - apply_global(correction, velocity)
    source = with_halo(remaining, (("gx", 0), ("gy", 1)), DEPTH)
    estimate = chebyshev(source, wide_velocity, inside)
    return correction + estimate[DEPTH : DEPTH + size_x, DEPTH : DEPTH + size_y]


def local(right_side, velocity, deflation, inverse_rows):
    size_x, size_y, size_z = right_side.shape
    wide_velocity = with_halo(velocity, (("gx", 1), ("gy", 2)), DEPTH)
    rows_x = lax.axis_index("gx") * size_x - DEPTH + lax.iota(jnp.int32, size_x + 2 * DEPTH)
    rows_y = lax.axis_index("gy") * size_y - DEPTH + lax.iota(jnp.int32, size_y + 2 * DEPTH)
    inside_x = ((rows_x >= 0) & (rows_x < size_x * lax.axis_size("gx"))).astype(jnp.float32)
    inside_y = ((rows_y >= 0) & (rows_y < size_y * lax.axis_size("gy"))).astype(jnp.float32)
    inside = inside_x[:, None, None] * inside_y[None, :, None]
    flat_vectors = deflation.reshape(KD, -1)
    rho_now = lax.psum(jnp.sum(right_side * right_side), ("gx", "gy"))
    search = precondition(right_side, velocity, wide_velocity, flat_vectors, inverse_rows, inside)
    image = apply_global(search, velocity)
    denominator = lax.psum(jnp.sum(right_side * image), ("gx", "gy"))
    alpha_step = rho_now / denominator
    middle = right_side - alpha_step * image
    smoothed = precondition(middle, velocity, wide_velocity, flat_vectors, inverse_rows, inside)
    turned = apply_global(smoothed, velocity)
    cross, square = lax.psum((jnp.sum(turned * middle), jnp.sum(turned * turned)), ("gx", "gy"))
    omega_step = cross / square
    solution_field = alpha_step * search + omega_step * smoothed
    return (solution_field, middle - omega_step * turned)


def solution(mesh):
    return jax.shard_map(
        local,
        mesh=mesh,
        in_specs=(
            P("gx", "gy", None),
            P(None, "gx", "gy", None),
            P(None, "gx", "gy", None),
            P(("gx", "gy"), None),
        ),
        out_specs=(P("gx", "gy", None), P("gx", "gy", None)),
        check_vma=False,
    )
```

profile of v0, /device:TPU:1, one launch (start us, length us, event | category | flops | bytes accessed | tf_op | source)
XLA Modules:
  0.0 445.5 jit_solution(6390966304339603937)
XLA Ops:
  1.7 2.8 fusion.8
  4.8 81.3 %all-reduce.10 = f32[8192]{0:T(1024)} all-reduce(f32[8192]{0:T(1024)S(1)} %dynamic-update-slice), channel_id=1, replica_groups=mesh['gx'=8,'gy'=32] {'gx','gy'}, use_global_device_ids=true, to_apply=%add.10 | all-reduce | flops 8192 | bytes 65536
  89.1 1.9 collective-permute-start.5
  91.0 2.4 collective-permute-start.4
  93.5 3.2 collective-permute-start
  96.6 1.9 collective-permute-start.1
  100.0 4.0 collective-permute-start.7
  105.2 4.8 %collective-permute-start.8 = (f32[2,16,256]{2,1,0:T(8,128)S(1)}, f32[2,16,256]{2,1,0:T(8,128)S(1)}, u32[]{:S(2)}, u32[]{:S(2)}) collective-permute-start(f32[2,16,256]{2,1,0:T(8,128)S(1)} %get-tuple-element.52), channel_id=1, source_target_pairs={{0,32},{32,64},{64,96},{96,128},{128,160},{160,192},{192,224},{1,3... | collective-permute-start | bytes 98312 | tf_op jit(solution)/shard_map/ppermute | solution.py:18
  110.0 1.9 collective-permute-start.9
  112.1 3.9 collective-permute-start.2
  117.4 4.0 collective-permute-start.10
  122.9 3.0 collective-permute-done.11
  127.3 1.9 collective-permute-start.12
  129.3 5.6 %collective-permute-start.13 = (f32[1,16,256]{2,1,0:T(8,128)S(1)}, f32[1,16,256]{2,1,0:T(8,128)S(1)}, u32[]{:S(2)}, u32[]{:S(2)}) collective-permute-start(f32[1,16,256]{2,1,0:T(8,128)S(1)} %get-tuple-element.50), channel_id=1, source_target_pairs={{0,32},{32,64},{64,96},{96,128},{128,160},{160,192},{192,224},{1,3... | collective-permute-start | bytes 49160 | tf_op jit(solution)/shard_map/ppermute | solution.py:18
  137.1 4.0 collective-permute-start.15
  142.8 87.5 %all-reduce.13 = (f32[]{:T(128)}, f32[]{:T(128)}) all-reduce(f32[]{:T(128)} %get-tuple-element.5, f32[]{:T(128)} %get-tuple-element.4), channel_id=1, replica_groups=mesh['gx'=8,'gy'=32] {'gx','gy'}, use_global_device_ids=true, to_apply=%region_1.0 | all-reduce | flops 2 | bytes 16 | tf_op jit(solution)/shard_map/psum | solution.py:89
  231.8 3.0 fusion.11
  235.0 73.9 %all-reduce.11 = f32[8192]{0:T(1024)S(1)} all-reduce(f32[8192]{0:T(1024)S(1)} %dynamic-update-slice.1), channel_id=1, replica_groups=mesh['gx'=8,'gy'=32] {'gx','gy'}, use_global_device_ids=true, to_apply=%add.11 | all-reduce | flops 8192 | bytes 65536
  309.8 2.0 fusion.132
  311.8 2.9 collective-permute-start.17
  314.8 1.9 collective-permute-start.16
  316.8 3.1 collective-permute-done.16
  321.2 4.0 collective-permute-start.19
  326.4 3.1 collective-permute-start.20
  329.4 1.9 collective-permute-start.21
  331.4 3.3 collective-permute-done.21
  334.7 3.9 collective-permute-start.22
  339.9 3.3 collective-permute-done.23
  345.5 1.9 collective-permute-start.24
  347.4 3.6 collective-permute-start.25
  353.3 4.0 collective-permute-start.27
  359.0 84.4 %all-reduce.12 = (f32[]{:T(128)}, f32[]{:T(128)}) all-reduce(f32[]{:T(128)} %get-tuple-element.3, f32[]{:T(128)} %get-tuple-element.2), channel_id=1, replica_groups=mesh['gx'=8,'gy'=32] {'gx','gy'}, use_global_device_ids=true, to_apply=%region_5.6 | all-reduce | flops 2 | bytes 16 | tf_op jit(solution)/shard_map/psum | solution.py:97
  (109 shorter events, 27.0 us)
Async XLA Ops:
  0.6 86.7 %copy-start = (f32[32,8192]{1,0:T(8,128)S(1)}, f32[32,8192]{1,0:T(8,128)}, u32[]{:S(2)}) copy-start(f32[32,8192]{1,0:T(8,128)} %param.7) | copy-start | bytes 3145732
  0.6 85.5 %copy-start.3 = (bf16[32,8,16,256]{3,2,1,0:T(8,128)(2,1)S(1)}, bf16[32,8,16,256]{3,2,1,0:T(8,128)(2,1)}, u32[]{:S(2)}) copy-start(bf16[32,8,16,256]{3,2,1,0:T(8,128)(2,1)} %param.6) | copy-start | bytes 6291460
  87.3 6.1 %copy-start.2 = (f32[3,8,16,256]{3,2,1,0:T(8,128)S(1)}, f32[3,8,16,256]{3,2,1,0:T(8,128)}, u32[]{:S(2)}) copy-start(f32[3,8,16,256]{3,2,1,0:T(8,128)} %param.5) | copy-start | bytes 1179652
  88.3 16.8 %copy-start.4 = (f32[8,16,256]{2,1,0:T(8,128)S(1)}, f32[8,16,256]{2,1,0:T(8,128)}, u32[]{:S(2)}) copy-start(f32[8,16,256]{2,1,0:T(8,128)} %param.4) | copy-start | bytes 393220
  89.1 9.6 %collective-permute-start.5 = (f32[1,16,256]{2,1,0:T(8,128)S(1)}, f32[1,16,256]{2,1,0:T(8,128)S(1)}, u32[]{:S(2)}, u32[]{:S(2)}) collective-permute-start(f32[1,16,256]{2,1,0:T(8,128)S(1)} %slice.464), channel_id=1, source_target_pairs={{0,32},{32,64},{64,96},{96,128},{128,160},{160,192},{192,224},{1,3... | collective-permute-start | bytes 49160 | tf_op jit(solution)/shard_map/ppermute | solution.py:18
  91.0 7.7 %collective-permute-start.4 = (f32[1,16,256]{2,1,0:T(8,128)S(1)}, f32[1,16,256]{2,1,0:T(8,128)S(1)}, u32[]{:S(2)}, u32[]{:S(2)}) collective-permute-start(f32[1,16,256]{2,1,0:T(8,128)S(1)} %slice.461), channel_id=1, source_target_pairs={{32,0},{64,32},{96,64},{128,96},{160,128},{192,160},{224,192},{33,... | collective-permute-start | bytes 49160 | tf_op jit(solution)/shard_map/ppermute | solution.py:21
  93.5 18.5 %collective-permute-start = (f32[3,2,16,256]{3,2,1,0:T(8,128)S(1)}, f32[3,2,16,256]{3,2,1,0:T(8,128)S(1)}, u32[]{:S(2)}, u32[]{:S(2)}) collective-permute-start(f32[3,2,16,256]{3,2,1,0:T(8,128)S(1)} %get-tuple-element.31), channel_id=1, source_target_pairs={{0,32},{32,64},{64,96},{96,128},{128,160},{160,192},{192,224},{1,3... | collective-permute-start | bytes 294920 | tf_op jit(solution)/shard_map/ppermute | solution.py:18
  96.6 15.4 %collective-permute-start.1 = (f32[3,2,16,256]{3,2,1,0:T(8,128)S(1)}, f32[3,2,16,256]{3,2,1,0:T(8,128)S(1)}, u32[]{:S(2)}, u32[]{:S(2)}) collective-permute-start(f32[3,2,16,256]{3,2,1,0:T(8,128)S(1)} %get-tuple-element.30), channel_id=1, source_target_pairs={{32,0},{64,32},{96,64},{128,96},{160,128},{192,160},{224,192},{33,... | collective-permute-start | bytes 294920 | tf_op jit(solution)/shard_map/ppermute | solution.py:21
  98.7 5.4 %collective-permute-start.6 = (f32[10,1,256]{2,1,0:T(1,128)S(1)}, f32[10,1,256]{2,1,0:T(1,128)S(1)}, u32[]{:S(2)}, u32[]{:S(2)}) collective-permute-start(f32[10,1,256]{2,1,0:T(1,128)S(1)} %get-tuple-element.43), channel_id=1, source_target_pairs={{1,0},{2,1},{3,2},{4,3},{5,4},{6,5},{7,6},{8,7},{9,8},{10,9},{11,1... | collective-permute-start | bytes 30728 | tf_op jit(solution)/shard_map/ppermute | solution.py:21
  100.0 4.8 %collective-permute-start.7 = (f32[10,1,256]{2,1,0:T(1,128)S(1)}, f32[10,1,256]{2,1,0:T(1,128)S(1)}, u32[]{:S(2)}, u32[]{:S(2)}) collective-permute-start(f32[10,1,256]{2,1,0:T(1,128)S(1)} %get-tuple-element.42), channel_id=1, source_target_pairs={{0,1},{1,2},{2,3},{3,4},{4,5},{5,6},{6,7},{7,8},{8,9},{9,10},{10,1... | collective-permute-start | bytes 30728 | tf_op jit(solution)/shard_map/ppermute | solution.py:18
  105.2 12.1 %collective-permute-start.8 = (f32[2,16,256]{2,1,0:T(8,128)S(1)}, f32[2,16,256]{2,1,0:T(8,128)S(1)}, u32[]{:S(2)}, u32[]{:S(2)}) collective-permute-start(f32[2,16,256]{2,1,0:T(8,128)S(1)} %get-tuple-element.52), channel_id=1, source_target_pairs={{0,32},{32,64},{64,96},{96,128},{128,160},{160,192},{192,224},{1,3... | collective-permute-start | bytes 98312 | tf_op jit(solution)/shard_map/ppermute | solution.py:18
  110.0 7.3 %collective-permute-start.9 = (f32[2,16,256]{2,1,0:T(8,128)S(1)}, f32[2,16,256]{2,1,0:T(8,128)S(1)}, u32[]{:S(2)}, u32[]{:S(2)}) collective-permute-start(f32[2,16,256]{2,1,0:T(8,128)S(1)} %get-tuple-element.53), channel_id=1, source_target_pairs={{32,0},{64,32},{96,64},{128,96},{160,128},{192,160},{224,192},{33,... | collective-permute-start | bytes 98312 | tf_op jit(solution)/shard_map/ppermute | solution.py:21
  112.1 10.6 %collective-permute-start.2 = (f32[3,12,2,256]{3,2,1,0:T(2,128)S(1)}, f32[3,12,2,256]{3,2,1,0:T(2,128)S(1)}, u32[]{:S(2)}, u32[]{:S(2)}) collective-permute-start(f32[3,12,2,256]{3,2,1,0:T(2,128)S(1)} %get-tuple-element.28), channel_id=1, source_target_pairs={{0,1},{1,2},{2,3},{3,4},{4,5},{5,6},{6,7},{7,8},{8,9},{9,10},{10,1... | collective-permute-start | bytes 221192 | tf_op jit(solution)/shard_map/ppermute | solution.py:18
  116.0 6.7 %collective-permute-start.3 = (f32[3,12,2,256]{3,2,1,0:T(2,128)S(1)}, f32[3,12,2,256]{3,2,1,0:T(2,128)S(1)}, u32[]{:S(2)}, u32[]{:S(2)}) collective-permute-start(f32[3,12,2,256]{3,2,1,0:T(2,128)S(1)} %get-tuple-element.29), channel_id=1, source_target_pairs={{1,0},{2,1},{3,2},{4,3},{5,4},{6,5},{7,6},{8,7},{9,8},{10,9},{11,1... | collective-permute-start | bytes 221192 | tf_op jit(solution)/shard_map/ppermute | solution.py:21
  117.4 5.5 %collective-permute-start.10 = (f32[12,2,256]{2,1,0:T(2,128)S(1)}, f32[12,2,256]{2,1,0:T(2,128)S(1)}, u32[]{:S(2)}, u32[]{:S(2)}) collective-permute-start(f32[12,2,256]{2,1,0:T(2,128)S(1)} %get-tuple-element.34), channel_id=1, source_target_pairs={{0,1},{1,2},{2,3},{3,4},{4,5},{5,6},{6,7},{7,8},{8,9},{9,10},{10,1... | collective-permute-start | bytes 73736 | tf_op jit(solution)/shard_map/ppermute | solution.py:18
  121.4 4.6 %collective-permute-start.11 = (f32[12,2,256]{2,1,0:T(2,128)S(1)}, f32[12,2,256]{2,1,0:T(2,128)S(1)}, u32[]{:S(2)}, u32[]{:S(2)}) collective-permute-start(f32[12,2,256]{2,1,0:T(2,128)S(1)} %get-tuple-element.35), channel_id=1, source_target_pairs={{1,0},{2,1},{3,2},{4,3},{5,4},{6,5},{7,6},{8,7},{9,8},{10,9},{11,1... | collective-permute-start | bytes 73736 | tf_op jit(solution)/shard_map/ppermute | solution.py:21
  127.3 7.6 %collective-permute-start.12 = (f32[1,16,256]{2,1,0:T(8,128)S(1)}, f32[1,16,256]{2,1,0:T(8,128)S(1)}, u32[]{:S(2)}, u32[]{:S(2)}) collective-permute-start(f32[1,16,256]{2,1,0:T(8,128)S(1)} %get-tuple-element.51), channel_id=1, source_target_pairs={{32,0},{64,32},{96,64},{128,96},{160,128},{192,160},{224,192},{33,... | collective-permute-start | bytes 49160 | tf_op jit(solution)/shard_map/ppermute | solution.py:21
  129.3 6.5 %collective-permute-start.13 = (f32[1,16,256]{2,1,0:T(8,128)S(1)}, f32[1,16,256]{2,1,0:T(8,128)S(1)}, u32[]{:S(2)}, u32[]{:S(2)}) collective-permute-start(f32[1,16,256]{2,1,0:T(8,128)S(1)} %get-tuple-element.50), channel_id=1, source_target_pairs={{0,32},{32,64},{64,96},{96,128},{128,160},{160,192},{192,224},{1,3... | collective-permute-start | bytes 49160 | tf_op jit(solution)/shard_map/ppermute | solution.py:18
  135.8 5.3 %collective-permute-start.14 = (f32[10,1,256]{2,1,0:T(1,128)S(1)}, f32[10,1,256]{2,1,0:T(1,128)S(1)}, u32[]{:S(2)}, u32[]{:S(2)}) collective-permute-start(f32[10,1,256]{2,1,0:T(1,128)S(1)} %get-tuple-element.41), channel_id=1, source_target_pairs={{1,0},{2,1},{3,2},{4,3},{5,4},{6,5},{7,6},{8,7},{9,8},{10,9},{11,1... | collective-permute-start | bytes 30728 | tf_op jit(solution)/shard_map/ppermute | solution.py:21
  137.1 4.8 %collective-permute-start.15 = (f32[10,1,256]{2,1,0:T(1,128)S(1)}, f32[10,1,256]{2,1,0:T(1,128)S(1)}, u32[]{:S(2)}, u32[]{:S(2)}) collective-permute-start(f32[10,1,256]{2,1,0:T(1,128)S(1)} %get-tuple-element.40), channel_id=1, source_target_pairs={{0,1},{1,2},{2,3},{3,4},{4,5},{5,6},{6,7},{7,8},{8,9},{9,10},{10,1... | collective-permute-start | bytes 30728 | tf_op jit(solution)/shard_map/ppermute | solution.py:18
  311.8 4.9 %collective-permute-start.17 = (f32[1,16,256]{2,1,0:T(8,128)S(1)}, f32[1,16,256]{2,1,0:T(8,128)S(1)}, u32[]{:S(2)}, u32[]{:S(2)}) collective-permute-start(f32[1,16,256]{2,1,0:T(8,128)S(1)} %slice.509), channel_id=1, source_target_pairs={{0,32},{32,64},{64,96},{96,128},{128,160},{160,192},{192,224},{1,3... | collective-permute-start | bytes 49160 | tf_op jit(solution)/shard_map/ppermute | solution.py:18
  314.8 5.1 %collective-permute-start.16 = (f32[1,16,256]{2,1,0:T(8,128)S(1)}, f32[1,16,256]{2,1,0:T(8,128)S(1)}, u32[]{:S(2)}, u32[]{:S(2)}) collective-permute-start(f32[1,16,256]{2,1,0:T(8,128)S(1)} %slice.506), channel_id=1, source_target_pairs={{32,0},{64,32},{96,64},{128,96},{160,128},{192,160},{224,192},{33,... | collective-permute-start | bytes 49160 | tf_op jit(solution)/shard_map/ppermute | solution.py:21
  319.9 5.3 %collective-permute-start.18 = (f32[10,1,256]{2,1,0:T(1,128)S(1)}, f32[10,1,256]{2,1,0:T(1,128)S(1)}, u32[]{:S(2)}, u32[]{:S(2)}) collective-permute-start(f32[10,1,256]{2,1,0:T(1,128)S(1)} %get-tuple-element.39), channel_id=1, source_target_pairs={{1,0},{2,1},{3,2},{4,3},{5,4},{6,5},{7,6},{8,7},{9,8},{10,9},{11,1... | collective-permute-start | bytes 30728 | tf_op jit(solution)/shard_map/ppermute | solution.py:21
  321.2 4.8 %collective-permute-start.19 = (f32[10,1,256]{2,1,0:T(1,128)S(1)}, f32[10,1,256]{2,1,0:T(1,128)S(1)}, u32[]{:S(2)}, u32[]{:S(2)}) collective-permute-start(f32[10,1,256]{2,1,0:T(1,128)S(1)} %get-tuple-element.38), channel_id=1, source_target_pairs={{0,1},{1,2},{2,3},{3,4},{4,5},{5,6},{6,7},{7,8},{8,9},{9,10},{10,1... | collective-permute-start | bytes 30728 | tf_op jit(solution)/shard_map/ppermute | solution.py:18
  326.4 5.0 %collective-permute-start.20 = (f32[2,16,256]{2,1,0:T(8,128)S(1)}, f32[2,16,256]{2,1,0:T(8,128)S(1)}, u32[]{:S(2)}, u32[]{:S(2)}) collective-permute-start(f32[2,16,256]{2,1,0:T(8,128)S(1)} %get-tuple-element.46), channel_id=1, source_target_pairs={{0,32},{32,64},{64,96},{96,128},{128,160},{160,192},{192,224},{1,3... | collective-permute-start | bytes 98312 | tf_op jit(solution)/shard_map/ppermute | solution.py:18
  329.4 5.2 %collective-permute-start.21 = (f32[2,16,256]{2,1,0:T(8,128)S(1)}, f32[2,16,256]{2,1,0:T(8,128)S(1)}, u32[]{:S(2)}, u32[]{:S(2)}) collective-permute-start(f32[2,16,256]{2,1,0:T(8,128)S(1)} %get-tuple-element.47), channel_id=1, source_target_pairs={{32,0},{64,32},{96,64},{128,96},{160,128},{192,160},{224,192},{33,... | collective-permute-start | bytes 98312 | tf_op jit(solution)/shard_map/ppermute | solution.py:21
  334.7 5.2 %collective-permute-start.22 = (f32[12,2,256]{2,1,0:T(2,128)S(1)}, f32[12,2,256]{2,1,0:T(2,128)S(1)}, u32[]{:S(2)}, u32[]{:S(2)}) collective-permute-start(f32[12,2,256]{2,1,0:T(2,128)S(1)} %get-tuple-element.32), channel_id=1, source_target_pairs={{0,1},{1,2},{2,3},{3,4},{4,5},{5,6},{6,7},{7,8},{8,9},{9,10},{10,1... | collective-permute-start | bytes 73736 | tf_op jit(solution)/shard_map/ppermute | solution.py:18
  338.6 4.6 %collective-permute-start.23 = (f32[12,2,256]{2,1,0:T(2,128)S(1)}, f32[12,2,256]{2,1,0:T(2,128)S(1)}, u32[]{:S(2)}, u32[]{:S(2)}) collective-permute-start(f32[12,2,256]{2,1,0:T(2,128)S(1)} %get-tuple-element.33), channel_id=1, source_target_pairs={{1,0},{2,1},{3,2},{4,3},{5,4},{6,5},{7,6},{8,7},{9,8},{10,9},{11,1... | collective-permute-start | bytes 73736 | tf_op jit(solution)/shard_map/ppermute | solution.py:21
  345.5 5.6 %collective-permute-start.24 = (f32[1,16,256]{2,1,0:T(8,128)S(1)}, f32[1,16,256]{2,1,0:T(8,128)S(1)}, u32[]{:S(2)}, u32[]{:S(2)}) collective-permute-start(f32[1,16,256]{2,1,0:T(8,128)S(1)} %get-tuple-element.45), channel_id=1, source_target_pairs={{32,0},{64,32},{96,64},{128,96},{160,128},{192,160},{224,192},{33,... | collective-permute-start | bytes 49160 | tf_op jit(solution)/shard_map/ppermute | solution.py:21
  347.4 4.5 %collective-permute-start.25 = (f32[1,16,256]{2,1,0:T(8,128)S(1)}, f32[1,16,256]{2,1,0:T(8,128)S(1)}, u32[]{:S(2)}, u32[]{:S(2)}) collective-permute-start(f32[1,16,256]{2,1,0:T(8,128)S(1)} %get-tuple-element.44), channel_id=1, source_target_pairs={{0,32},{32,64},{64,96},{96,128},{128,160},{160,192},{192,224},{1,3... | collective-permute-start | bytes 49160 | tf_op jit(solution)/shard_map/ppermute | solution.py:18
  352.0 5.3 %collective-permute-start.26 = (f32[10,1,256]{2,1,0:T(1,128)S(1)}, f32[10,1,256]{2,1,0:T(1,128)S(1)}, u32[]{:S(2)}, u32[]{:S(2)}) collective-permute-start(f32[10,1,256]{2,1,0:T(1,128)S(1)} %get-tuple-element.37), channel_id=1, source_target_pairs={{1,0},{2,1},{3,2},{4,3},{5,4},{6,5},{7,6},{8,7},{9,8},{10,9},{11,1... | collective-permute-start | bytes 30728 | tf_op jit(solution)/shard_map/ppermute | solution.py:21
  353.3 4.8 %collective-permute-start.27 = (f32[10,1,256]{2,1,0:T(1,128)S(1)}, f32[10,1,256]{2,1,0:T(1,128)S(1)}, u32[]{:S(2)}, u32[]{:S(2)}) collective-permute-start(f32[10,1,256]{2,1,0:T(1,128)S(1)} %get-tuple-element.36), channel_id=1, source_target_pairs={{0,1},{1,2},{2,3},{3,4},{4,5},{5,6},{6,7},{7,8},{8,9},{9,10},{10,1... | collective-permute-start | bytes 30728 | tf_op jit(solution)/shard_map/ppermute | solution.py:18
  (3 other events, 6.9 us)
where the time goes:
time: 447 us; the launch traced here: 446 us
  blocking collectives  327 us (73%)
  starting transfers between devices  75.8 us (17%)
  waiting for transfers between devices  17.4 us (4%)
  matrix products  10 us (2%)
  other arithmetic  8.6 us (2%)
    unnamed x2, blocking collectives  155 us
    psum x1, blocking collectives, local(): rho_now = lax.psum(jnp.sum(right_side * right_side), ('gx', 'gy'))  87.5 us
    psum x1, blocking collectives, local(): lax.psum((jnp.sum(turned * middle), jnp.sum(turned * turned)), ('gx', 'gy'))  84.4 us
    ppermute x14, starting transfers between devices, with_halo(): lax.ppermute(lax.slice_in_dim(block, block.shape[dim] - width, None, axis...  52.8 us
    ppermute x14, starting transfers between devices, with_halo(): lax.ppermute(lax.slice_in_dim(block, 0, width, axis=dim), axis, backward)  23 us
    ppermute x14, waiting for transfers between devices, with_halo(): lax.ppermute(lax.slice_in_dim(block, 0, width, axis=dim), axis, backward)  12.7 us
  transfers between devices with their start and end apart: 28, of which 10 were waited for; matrix products, arithmetic and copies ran while one was open for 0% of the time, Pallas kernels for 0%

commit v1 on v0

--- a/solution.py
+++ b/solution.py
@@ -94,7 +94,10 @@
     middle = right_side - alpha_step * image
     smoothed = precondition(middle, velocity, wide_velocity, flat_vectors, inverse_rows, inside)
     turned = apply_global(smoothed, velocity)
-    cross, square = lax.psum((jnp.sum(turned * middle), jnp.sum(turned * turned)), ("gx", "gy"))
+    cross, square = lax.psum(
+        lax.psum((jnp.sum(turned * middle), jnp.sum(turned * turned)), axis_name="gx"),
+        axis_name="gy",
+    )
     omega_step = cross / square
     solution_field = alpha_step * search + omega_step * smoothed
     return (solution_field, middle - omega_step * turned)

time: 447 us -> 448 us (level)
  the two profiles are of different devices: /device:TPU:1 before, /device:TPU:8 now
where the time goes in v1:
time: 448 us; the launch traced here: 447 us
  blocking collectives  321 us (72%)
  starting transfers between devices  76.7 us (17%)
  waiting for transfers between devices  22.4 us (5%)
  matrix products  10 us (2%)
  other arithmetic  8.52 us (2%)
    unnamed x2, blocking collectives  153 us
    psum x1, blocking collectives, local(): rho_now = lax.psum(jnp.sum(right_side * right_side), ('gx', 'gy'))  83.9 us
    psum x1, blocking collectives, local(): lax.psum(lax.psum((jnp.sum(turned * middle), jnp.sum(turned * turned)), a...  73 us
    ppermute x14, starting transfers between devices, with_halo(): lax.ppermute(lax.slice_in_dim(block, block.shape[dim] - width, None, axis...  45.2 us
    ppermute x14, starting transfers between devices, with_halo(): lax.ppermute(lax.slice_in_dim(block, 0, width, axis=dim), axis, backward)  31.5 us
    ppermute x14, waiting for transfers between devices, with_halo(): lax.ppermute(lax.slice_in_dim(block, 0, width, axis=dim), axis, backward)  11.4 us
    ppermute x14, waiting for transfers between devices, with_halo(): lax.ppermute(lax.slice_in_dim(block, block.shape[dim] - width, None, axis...  11.1 us
    psum x1, blocking collectives, local(): lax.psum((jnp.sum(turned * middle), jnp.sum(turned * turned)), axis_name=...  10.6 us
  transfers between devices with their start and end apart: 28, of which 11 were waited for; matrix products, arithmetic and copies ran while one was open for 0% of the time, Pallas kernels for 0%

profile of v1, /device:TPU:8, one launch (start us, length us, event | category | flops | bytes accessed | tf_op | source)
XLA Modules:
  0.0 446.6 jit_solution(7868631924875112714)
XLA Ops:
  1.7 2.8 fusion.8
  4.7 78.6 %all-reduce.10 = f32[8192]{0:T(1024)S(1)} all-reduce(f32[8192]{0:T(1024)S(1)} %dynamic-update-slice), channel_id=1, replica_groups=mesh['gx'=8,'gy'=32] {'gx','gy'}, use_global_device_ids=true, to_apply=%add.10 | all-reduce | flops 8192 | bytes 65536
  83.4 2.8 copy.11
  87.9 1.9 collective-permute-start.5
  89.8 3.7 collective-permute-start.4
  93.6 1.9 collective-permute-start
  95.5 3.6 collective-permute-start.1
  100.7 4.5 %collective-permute-start.7 = (f32[10,1,256]{2,1,0:T(1,128)S(1)}, f32[10,1,256]{2,1,0:T(1,128)S(1)}, u32[]{:S(2)}, u32[]{:S(2)}) collective-permute-start(f32[10,1,256]{2,1,0:T(1,128)S(1)} %get-tuple-element.44), channel_id=1, source_target_pairs={{0,1},{1,2},{2,3},{3,4},{4,5},{5,6},{6,7},{7,8},{8,9},{9,10},{10,1... | collective-permute-start | bytes 30728 | tf_op jit(solution)/shard_map/ppermute | solution.py:18
  107.0 1.9 collective-permute-start.8
  108.9 3.6 collective-permute-start.9
  112.7 4.2 collective-permute-start.2
  118.3 4.5 %collective-permute-start.10 = (f32[12,2,256]{2,1,0:T(2,128)S(1)}, f32[12,2,256]{2,1,0:T(2,128)S(1)}, u32[]{:S(2)}, u32[]{:S(2)}) collective-permute-start(f32[12,2,256]{2,1,0:T(2,128)S(1)} %get-tuple-element.36), channel_id=1, source_target_pairs={{0,1},{1,2},{2,3},{3,4},{4,5},{5,6},{6,7},{7,8},{8,9},{9,10},{10,1... | collective-permute-start | bytes 73736 | tf_op jit(solution)/shard_map/ppermute | solution.py:18
  124.4 4.2 collective-permute-done.11
  130.0 1.9 collective-permute-start.12
  131.9 2.4 collective-permute-start.13
  134.3 2.6 collective-permute-done.13
  138.3 4.5 %collective-permute-start.15 = (f32[10,1,256]{2,1,0:T(1,128)S(1)}, f32[10,1,256]{2,1,0:T(1,128)S(1)}, u32[]{:S(2)}, u32[]{:S(2)}) collective-permute-start(f32[10,1,256]{2,1,0:T(1,128)S(1)} %get-tuple-element.42), channel_id=1, source_target_pairs={{0,1},{1,2},{2,3},{3,4},{4,5},{5,6},{6,7},{7,8},{8,9},{9,10},{10,1... | collective-permute-start | bytes 30728 | tf_op jit(solution)/shard_map/ppermute | solution.py:18
  145.2 83.9 %all-reduce.12 = (f32[]{:T(128)}, f32[]{:T(128)}) all-reduce(f32[]{:T(128)} %get-tuple-element.5, f32[]{:T(128)} %get-tuple-element.4), channel_id=1, replica_groups=mesh['gx'=8,'gy'=32] {'gx','gy'}, use_global_device_ids=true, to_apply=%region_1.0 | all-reduce | flops 2 | bytes 16 | tf_op jit(solution)/shard_map/psum | solution.py:89
  230.4 3.0 fusion.11
  233.7 74.5 %all-reduce.11 = f32[8192]{0:T(1024)S(1)} all-reduce(f32[8192]{0:T(1024)S(1)} %dynamic-update-slice.1), channel_id=1, replica_groups=mesh['gx'=8,'gy'=32] {'gx','gy'}, use_global_device_ids=true, to_apply=%add.11 | all-reduce | flops 8192 | bytes 65536
  309.1 2.0 fusion.132
  313.1 3.6 collective-permute-start.16
  319.5 4.5 %collective-permute-start.19 = (f32[10,1,256]{2,1,0:T(1,128)S(1)}, f32[10,1,256]{2,1,0:T(1,128)S(1)}, u32[]{:S(2)}, u32[]{:S(2)}) collective-permute-start(f32[10,1,256]{2,1,0:T(1,128)S(1)} %get-tuple-element.40), channel_id=1, source_target_pairs={{0,1},{1,2},{2,3},{3,4},{4,5},{5,6},{6,7},{7,8},{8,9},{9,10},{10,1... | collective-permute-start | bytes 30728 | tf_op jit(solution)/shard_map/ppermute | solution.py:18
  327.8 3.6 collective-permute-start.21
  333.0 4.2 collective-permute-start.22
  338.7 4.2 collective-permute-done.23
  345.3 2.2 collective-permute-start.24
  347.5 2.1 collective-permute-start.25
  349.6 2.9 collective-permute-done.25
  353.9 4.5 %collective-permute-start.27 = (f32[10,1,256]{2,1,0:T(1,128)S(1)}, f32[10,1,256]{2,1,0:T(1,128)S(1)}, u32[]{:S(2)}, u32[]{:S(2)}) collective-permute-start(f32[10,1,256]{2,1,0:T(1,128)S(1)} %get-tuple-element.38), channel_id=1, source_target_pairs={{0,1},{1,2},{2,3},{3,4},{4,5},{5,6},{6,7},{7,8},{8,9},{9,10},{10,1... | collective-permute-start | bytes 30728 | tf_op jit(solution)/shard_map/ppermute | solution.py:18
  360.8 10.6 %all-reduce.14 = (f32[]{:T(128)}, f32[]{:T(128)}) all-reduce(f32[]{:T(128)} %get-tuple-element.3, f32[]{:T(128)} %get-tuple-element.2), channel_id=1, replica_groups=mesh['gx'=8,'gy'=32] {'gx'}, use_global_device_ids=true, to_apply=%region_5.6 | all-reduce | flops 2 | bytes 16 | tf_op jit(solution)/shard_map/psum | solution.py:98
  371.4 73.0 %all-reduce.13 = (f32[]{:T(128)}, f32[]{:T(128)}) all-reduce(f32[]{:T(128)} %get-tuple-element.10, f32[]{:T(128)} %get-tuple-element.11), channel_id=1, replica_groups=mesh['gx'=8,'gy'=32] {'gy'}, use_global_device_ids=true, to_apply=%region_6.7 | all-reduce | flops 2 | bytes 16 | tf_op jit(solution)/shard_map/psum | solution.py:97
  (106 shorter events, 33.4 us)
Async XLA Ops:
  0.6 85.5 %copy-start = (f32[32,8192]{1,0:T(8,128)S(1)}, f32[32,8192]{1,0:T(8,128)}, u32[]{:S(2)}) copy-start(f32[32,8192]{1,0:T(8,128)} %param.7) | copy-start | bytes 3145732
  86.1 7.4 %copy-start.2 = (f32[3,8,16,256]{3,2,1,0:T(8,128)S(1)}, f32[3,8,16,256]{3,2,1,0:T(8,128)}, u32[]{:S(2)}) copy-start(f32[3,8,16,256]{3,2,1,0:T(8,128)} %param.5) | copy-start | bytes 1179652
  87.1 19.7 %copy-start.3 = (f32[8,16,256]{2,1,0:T(8,128)S(1)}, f32[8,16,256]{2,1,0:T(8,128)}, u32[]{:S(2)}) copy-start(f32[8,16,256]{2,1,0:T(8,128)} %param.4) | copy-start | bytes 393220
  87.9 11.4 %collective-permute-start.5 = (f32[1,16,256]{2,1,0:T(8,128)S(1)}, f32[1,16,256]{2,1,0:T(8,128)S(1)}, u32[]{:S(2)}, u32[]{:S(2)}) collective-permute-start(f32[1,16,256]{2,1,0:T(8,128)S(1)} %slice.464), channel_id=1, source_target_pairs={{0,32},{32,64},{64,96},{96,128},{128,160},{160,192},{192,224},{1,3... | collective-permute-start | bytes 49160 | tf_op jit(solution)/shard_map/ppermute | solution.py:18
  89.8 9.5 %collective-permute-start.4 = (f32[1,16,256]{2,1,0:T(8,128)S(1)}, f32[1,16,256]{2,1,0:T(8,128)S(1)}, u32[]{:S(2)}, u32[]{:S(2)}) collective-permute-start(f32[1,16,256]{2,1,0:T(8,128)S(1)} %slice.461), channel_id=1, source_target_pairs={{32,0},{64,32},{96,64},{128,96},{160,128},{192,160},{224,192},{33,... | collective-permute-start | bytes 49160 | tf_op jit(solution)/shard_map/ppermute | solution.py:21
  93.6 19.0 %collective-permute-start = (f32[3,2,16,256]{3,2,1,0:T(8,128)S(1)}, f32[3,2,16,256]{3,2,1,0:T(8,128)S(1)}, u32[]{:S(2)}, u32[]{:S(2)}) collective-permute-start(f32[3,2,16,256]{3,2,1,0:T(8,128)S(1)} %get-tuple-element.33), channel_id=1, source_target_pairs={{0,32},{32,64},{64,96},{96,128},{128,160},{160,192},{192,224},{1,3... | collective-permute-start | bytes 294920 | tf_op jit(solution)/shard_map/ppermute | solution.py:18
  95.5 17.1 %collective-permute-start.1 = (f32[3,2,16,256]{3,2,1,0:T(8,128)S(1)}, f32[3,2,16,256]{3,2,1,0:T(8,128)S(1)}, u32[]{:S(2)}, u32[]{:S(2)}) collective-permute-start(f32[3,2,16,256]{3,2,1,0:T(8,128)S(1)} %get-tuple-element.32), channel_id=1, source_target_pairs={{32,0},{64,32},{96,64},{128,96},{160,128},{192,160},{224,192},{33,... | collective-permute-start | bytes 294920 | tf_op jit(solution)/shard_map/ppermute | solution.py:21
  99.4 6.0 %collective-permute-start.6 = (f32[10,1,256]{2,1,0:T(1,128)S(1)}, f32[10,1,256]{2,1,0:T(1,128)S(1)}, u32[]{:S(2)}, u32[]{:S(2)}) collective-permute-start(f32[10,1,256]{2,1,0:T(1,128)S(1)} %get-tuple-element.45), channel_id=1, source_target_pairs={{1,0},{2,1},{3,2},{4,3},{5,4},{6,5},{7,6},{8,7},{9,8},{10,9},{11,1... | collective-permute-start | bytes 30728 | tf_op jit(solution)/shard_map/ppermute | solution.py:21
  100.7 5.9 %collective-permute-start.7 = (f32[10,1,256]{2,1,0:T(1,128)S(1)}, f32[10,1,256]{2,1,0:T(1,128)S(1)}, u32[]{:S(2)}, u32[]{:S(2)}) collective-permute-start(f32[10,1,256]{2,1,0:T(1,128)S(1)} %get-tuple-element.44), channel_id=1, source_target_pairs={{0,1},{1,2},{2,3},{3,4},{4,5},{5,6},{6,7},{7,8},{8,9},{9,10},{10,1... | collective-permute-start | bytes 30728 | tf_op jit(solution)/shard_map/ppermute | solution.py:18
  107.0 11.2 %collective-permute-start.8 = (f32[2,16,256]{2,1,0:T(8,128)S(1)}, f32[2,16,256]{2,1,0:T(8,128)S(1)}, u32[]{:S(2)}, u32[]{:S(2)}) collective-permute-start(f32[2,16,256]{2,1,0:T(8,128)S(1)} %get-tuple-element.54), channel_id=1, source_target_pairs={{0,32},{32,64},{64,96},{96,128},{128,160},{160,192},{192,224},{1,3... | collective-permute-start | bytes 98312 | tf_op jit(solution)/shard_map/ppermute | solution.py:18
  108.9 9.3 %collective-permute-start.9 = (f32[2,16,256]{2,1,0:T(8,128)S(1)}, f32[2,16,256]{2,1,0:T(8,128)S(1)}, u32[]{:S(2)}, u32[]{:S(2)}) collective-permute-start(f32[2,16,256]{2,1,0:T(8,128)S(1)} %get-tuple-element.55), channel_id=1, source_target_pairs={{32,0},{64,32},{96,64},{128,96},{160,128},{192,160},{224,192},{33,... | collective-permute-start | bytes 98312 | tf_op jit(solution)/shard_map/ppermute | solution.py:21
  112.7 11.4 %collective-permute-start.2 = (f32[3,12,2,256]{3,2,1,0:T(2,128)S(1)}, f32[3,12,2,256]{3,2,1,0:T(2,128)S(1)}, u32[]{:S(2)}, u32[]{:S(2)}) collective-permute-start(f32[3,12,2,256]{3,2,1,0:T(2,128)S(1)} %get-tuple-element.30), channel_id=1, source_target_pairs={{0,1},{1,2},{2,3},{3,4},{4,5},{5,6},{6,7},{7,8},{8,9},{9,10},{10,1... | collective-permute-start | bytes 221192 | tf_op jit(solution)/shard_map/ppermute | solution.py:18
  116.9 7.2 %collective-permute-start.3 = (f32[3,12,2,256]{3,2,1,0:T(2,128)S(1)}, f32[3,12,2,256]{3,2,1,0:T(2,128)S(1)}, u32[]{:S(2)}, u32[]{:S(2)}) collective-permute-start(f32[3,12,2,256]{3,2,1,0:T(2,128)S(1)} %get-tuple-element.31), channel_id=1, source_target_pairs={{1,0},{2,1},{3,2},{4,3},{5,4},{6,5},{7,6},{8,7},{9,8},{10,9},{11,1... | collective-permute-start | bytes 221192 | tf_op jit(solution)/shard_map/ppermute | solution.py:21
  118.3 6.1 %collective-permute-start.10 = (f32[12,2,256]{2,1,0:T(2,128)S(1)}, f32[12,2,256]{2,1,0:T(2,128)S(1)}, u32[]{:S(2)}, u32[]{:S(2)}) collective-permute-start(f32[12,2,256]{2,1,0:T(2,128)S(1)} %get-tuple-element.36), channel_id=1, source_target_pairs={{0,1},{1,2},{2,3},{3,4},{4,5},{5,6},{6,7},{7,8},{8,9},{9,10},{10,1... | collective-permute-start | bytes 73736 | tf_op jit(solution)/shard_map/ppermute | solution.py:18
  122.8 5.7 %collective-permute-start.11 = (f32[12,2,256]{2,1,0:T(2,128)S(1)}, f32[12,2,256]{2,1,0:T(2,128)S(1)}, u32[]{:S(2)}, u32[]{:S(2)}) collective-permute-start(f32[12,2,256]{2,1,0:T(2,128)S(1)} %get-tuple-element.37), channel_id=1, source_target_pairs={{1,0},{2,1},{3,2},{4,3},{5,4},{6,5},{7,6},{8,7},{9,8},{10,9},{11,1... | collective-permute-start | bytes 73736 | tf_op jit(solution)/shard_map/ppermute | solution.py:21
  124.4 5.4 %copy-start.4 = (f32[12,20,256]{2,1,0:T(8,128)}, f32[12,20,256]{2,1,0:T(8,128)S(1)}, u32[]{:S(2)}) copy-start(f32[12,20,256]{2,1,0:T(8,128)S(1)} %get-tuple-element.21) | copy-start | bytes 737284
  130.0 4.3 collective-permute-start.12
  131.9 5.1 %collective-permute-start.13 = (f32[1,16,256]{2,1,0:T(8,128)S(1)}, f32[1,16,256]{2,1,0:T(8,128)S(1)}, u32[]{:S(2)}, u32[]{:S(2)}) collective-permute-start(f32[1,16,256]{2,1,0:T(8,128)S(1)} %get-tuple-element.52), channel_id=1, source_target_pairs={{0,32},{32,64},{64,96},{96,128},{128,160},{160,192},{192,224},{1,3... | collective-permute-start | bytes 49160 | tf_op jit(solution)/shard_map/ppermute | solution.py:18
  137.0 5.9 %collective-permute-start.14 = (f32[10,1,256]{2,1,0:T(1,128)S(1)}, f32[10,1,256]{2,1,0:T(1,128)S(1)}, u32[]{:S(2)}, u32[]{:S(2)}) collective-permute-start(f32[10,1,256]{2,1,0:T(1,128)S(1)} %get-tuple-element.43), channel_id=1, source_target_pairs={{1,0},{2,1},{3,2},{4,3},{5,4},{6,5},{7,6},{8,7},{9,8},{10,9},{11,1... | collective-permute-start | bytes 30728 | tf_op jit(solution)/shard_map/ppermute | solution.py:21
  138.3 5.9 %collective-permute-start.15 = (f32[10,1,256]{2,1,0:T(1,128)S(1)}, f32[10,1,256]{2,1,0:T(1,128)S(1)}, u32[]{:S(2)}, u32[]{:S(2)}) collective-permute-start(f32[10,1,256]{2,1,0:T(1,128)S(1)} %get-tuple-element.42), channel_id=1, source_target_pairs={{0,1},{1,2},{2,3},{3,4},{4,5},{5,6},{6,7},{7,8},{8,9},{9,10},{10,1... | collective-permute-start | bytes 30728 | tf_op jit(solution)/shard_map/ppermute | solution.py:18
  311.1 5.6 %collective-permute-start.17 = (f32[1,16,256]{2,1,0:T(8,128)S(1)}, f32[1,16,256]{2,1,0:T(8,128)S(1)}, u32[]{:S(2)}, u32[]{:S(2)}) collective-permute-start(f32[1,16,256]{2,1,0:T(8,128)S(1)} %slice.509), channel_id=1, source_target_pairs={{0,32},{32,64},{64,96},{96,128},{128,160},{160,192},{192,224},{1,3... | collective-permute-start | bytes 49160 | tf_op jit(solution)/shard_map/ppermute | solution.py:18
  313.1 5.1 %collective-permute-start.16 = (f32[1,16,256]{2,1,0:T(8,128)S(1)}, f32[1,16,256]{2,1,0:T(8,128)S(1)}, u32[]{:S(2)}, u32[]{:S(2)}) collective-permute-start(f32[1,16,256]{2,1,0:T(8,128)S(1)} %slice.506), channel_id=1, source_target_pairs={{32,0},{64,32},{96,64},{128,96},{160,128},{192,160},{224,192},{33,... | collective-permute-start | bytes 49160 | tf_op jit(solution)/shard_map/ppermute | solution.py:21
  318.2 5.9 %collective-permute-start.18 = (f32[10,1,256]{2,1,0:T(1,128)S(1)}, f32[10,1,256]{2,1,0:T(1,128)S(1)}, u32[]{:S(2)}, u32[]{:S(2)}) collective-permute-start(f32[10,1,256]{2,1,0:T(1,128)S(1)} %get-tuple-element.41), channel_id=1, source_target_pairs={{1,0},{2,1},{3,2},{4,3},{5,4},{6,5},{7,6},{8,7},{9,8},{10,9},{11,1... | collective-permute-start | bytes 30728 | tf_op jit(solution)/shard_map/ppermute | solution.py:21
  319.5 5.9 %collective-permute-start.19 = (f32[10,1,256]{2,1,0:T(1,128)S(1)}, f32[10,1,256]{2,1,0:T(1,128)S(1)}, u32[]{:S(2)}, u32[]{:S(2)}) collective-permute-start(f32[10,1,256]{2,1,0:T(1,128)S(1)} %get-tuple-element.40), channel_id=1, source_target_pairs={{0,1},{1,2},{2,3},{3,4},{4,5},{5,6},{6,7},{7,8},{8,9},{9,10},{10,1... | collective-permute-start | bytes 30728 | tf_op jit(solution)/shard_map/ppermute | solution.py:18
  325.8 5.6 %collective-permute-start.20 = (f32[2,16,256]{2,1,0:T(8,128)S(1)}, f32[2,16,256]{2,1,0:T(8,128)S(1)}, u32[]{:S(2)}, u32[]{:S(2)}) collective-permute-start(f32[2,16,256]{2,1,0:T(8,128)S(1)} %get-tuple-element.48), channel_id=1, source_target_pairs={{0,32},{32,64},{64,96},{96,128},{128,160},{160,192},{192,224},{1,3... | collective-permute-start | bytes 98312 | tf_op jit(solution)/shard_map/ppermute | solution.py:18
  327.8 5.2 %collective-permute-start.21 = (f32[2,16,256]{2,1,0:T(8,128)S(1)}, f32[2,16,256]{2,1,0:T(8,128)S(1)}, u32[]{:S(2)}, u32[]{:S(2)}) collective-permute-start(f32[2,16,256]{2,1,0:T(8,128)S(1)} %get-tuple-element.49), channel_id=1, source_target_pairs={{32,0},{64,32},{96,64},{128,96},{160,128},{192,160},{224,192},{33,... | collective-permute-start | bytes 98312 | tf_op jit(solution)/shard_map/ppermute | solution.py:21
  333.0 5.7 %collective-permute-start.22 = (f32[12,2,256]{2,1,0:T(2,128)S(1)}, f32[12,2,256]{2,1,0:T(2,128)S(1)}, u32[]{:S(2)}, u32[]{:S(2)}) collective-permute-start(f32[12,2,256]{2,1,0:T(2,128)S(1)} %get-tuple-element.34), channel_id=1, source_target_pairs={{0,1},{1,2},{2,3},{3,4},{4,5},{5,6},{6,7},{7,8},{8,9},{9,10},{10,1... | collective-permute-start | bytes 73736 | tf_op jit(solution)/shard_map/ppermute | solution.py:18
  337.2 5.7 %collective-permute-start.23 = (f32[12,2,256]{2,1,0:T(2,128)S(1)}, f32[12,2,256]{2,1,0:T(2,128)S(1)}, u32[]{:S(2)}, u32[]{:S(2)}) collective-permute-start(f32[12,2,256]{2,1,0:T(2,128)S(1)} %get-tuple-element.35), channel_id=1, source_target_pairs={{1,0},{2,1},{3,2},{4,3},{5,4},{6,5},{7,6},{8,7},{9,8},{10,9},{11,1... | collective-permute-start | bytes 73736 | tf_op jit(solution)/shard_map/ppermute | solution.py:21
  345.3 4.3 collective-permute-start.24
  347.5 5.1 %collective-permute-start.25 = (f32[1,16,256]{2,1,0:T(8,128)S(1)}, f32[1,16,256]{2,1,0:T(8,128)S(1)}, u32[]{:S(2)}, u32[]{:S(2)}) collective-permute-start(f32[1,16,256]{2,1,0:T(8,128)S(1)} %get-tuple-element.46), channel_id=1, source_target_pairs={{0,32},{32,64},{64,96},{96,128},{128,160},{160,192},{192,224},{1,3... | collective-permute-start | bytes 49160 | tf_op jit(solution)/shard_map/ppermute | solution.py:18
  352.6 5.9 %collective-permute-start.26 = (f32[10,1,256]{2,1,0:T(1,128)S(1)}, f32[10,1,256]{2,1,0:T(1,128)S(1)}, u32[]{:S(2)}, u32[]{:S(2)}) collective-permute-start(f32[10,1,256]{2,1,0:T(1,128)S(1)} %get-tuple-element.39), channel_id=1, source_target_pairs={{1,0},{2,1},{3,2},{4,3},{5,4},{6,5},{7,6},{8,7},{9,8},{10,9},{11,1... | collective-permute-start | bytes 30728 | tf_op jit(solution)/shard_map/ppermute | solution.py:21
  353.9 5.9 %collective-permute-start.27 = (f32[10,1,256]{2,1,0:T(1,128)S(1)}, f32[10,1,256]{2,1,0:T(1,128)S(1)}, u32[]{:S(2)}, u32[]{:S(2)}) collective-permute-start(f32[10,1,256]{2,1,0:T(1,128)S(1)} %get-tuple-element.38), channel_id=1, source_target_pairs={{0,1},{1,2},{2,3},{3,4},{4,5},{5,6},{6,7},{7,8},{8,9},{9,10},{10,1... | collective-permute-start | bytes 30728 | tf_op jit(solution)/shard_map/ppermute | solution.py:18
  (1 other events, 1.4 us)
